TPU v7x, 256 devices: a whole 4x4x8 slice. The times are simulated.
256 devices in a mesh: sec: 32 (over x, z), op: 8 (over y, core).
Axes of the slice: x: 4, y: 4, z: 8, core: 2. Of those that a mesh axis runs over, the one named last changes fastest.
Arguments:
- state_start: bfloat16 [64, 256, 256], P('sec'), may hold values from -60 to 60
- left_ops: bfloat16 [64, 64, 256, 256], P('op', 'sec'), may hold values from -0.375 to 0.375
- right_ops: bfloat16 [64, 64, 256, 256], P('op', 'sec'), may hold values from -0.046875 to 0.046875
- shift: float32 [64], P('sec'), may hold values from 0.2 to 2.2
- partner: int32 [64, 64], P('op', 'sec'), may hold values from 0 to 5
- kept: int32 [64], P('sec'), may hold values from 128 to 256
Outputs:
- state_final: bfloat16 [64, 256, 256], P('sec')
- new_ops: bfloat16 [64, 64, 256, 256], P('op', 'sec')
Inputs may be any that keep to these rules, and one draw needn't show every extreme that they name: `partner`: position in the window of 6 sector blocks.
All inputs are finite; a program needn't handle non-finite values.
Results may differ from a plain program's by a relative error of at most 0.015.
Values may be sent and summed in bfloat16 or wider, within the bound.
A program may use at most 64 MiB of HBM per device.

v0:
```python
import jax
import jax.numpy as jnp
from jax import lax
from jax.sharding import PartitionSpec as P

ITERS = 4
step_size = 0.5


def padded(cells, sides, width):
    for axis, dim in sides:
        count = lax.axis_size(axis)
        head = lax.slice_in_dim(cells, 0, width, axis=dim)
        tail = lax.slice_in_dim(cells, cells.shape[dim] - width, cells.shape[dim], axis=dim)
        cells = jnp.concatenate(
            [
                lax.ppermute(tail, axis, [(i, (i + 1) % count) for i in range(count)]),
                cells,
                lax.ppermute(head, axis, [((i + 1) % count, i) for i in range(count)]),
            ],
            axis=dim,
        )
    return cells


def shifted(block, axis, distance):
    devices = range(lax.axis_size(axis))
    route = [((i - distance) % len(devices), i) for i in devices]
    return lax.ppermute(block, axis, route)


def per_device(state_start, left_ops, right_ops, shift, partner, kept):
    sector_local = state_start.shape[0]
    width = state_start.shape[1]
    share_rows = width // lax.axis_size("op")
    share_start = lax.axis_index("op") * share_rows
    count = float(sector_local * lax.axis_size("sec") * width * width)
    shift_col = shift[:, None, None]
    state = state_start
    for iteration in range(ITERS):
        window = padded(state, (("sec", 0),), sector_local)
        sources = window[partner]
        halfway = jnp.einsum(
            "tbij,tbjk->tbik", left_ops, sources, preferred_element_type=jnp.float32
        ).astype(jnp.bfloat16)
        partial_sigma = jnp.einsum(
            "tbij,tbjk->bik", halfway, right_ops, preferred_element_type=jnp.float32
        )
        state_wide = state.astype(jnp.float32)
        state_part = lax.dynamic_slice_in_dim(state_wide, share_start, share_rows, 1)
        sigma = lax.psum(partial_sigma, "op") + shift_col * state_wide
        sigma_part = lax.dynamic_slice_in_dim(sigma, share_start, share_rows, 1)
        energy_sum, norm_sum, square_sum = lax.psum(
            (
                jnp.sum(state_part * sigma_part),
                jnp.sum(state_part * state_part),
                jnp.sum(sigma_part * sigma_part),
            ),
            ("sec", "op"),
        )
        ratio = energy_sum / norm_sum
        updated_part = state_part - step_size * (sigma_part - ratio * state_part)
        new_norm = lax.psum(jnp.sum(updated_part * updated_part), ("sec", "op"))
        factor = jnp.sqrt(count / new_norm)
        updated = state_wide - step_size * (sigma - ratio * state_wide)
        state = (updated * factor).astype(jnp.bfloat16)
    columns = jnp.arange(width, dtype=jnp.int32)
    keep_mask = (columns[None, :] < kept[:, None]).astype(jnp.bfloat16)
    kept_block = state * keep_mask[:, None, :]
    out_scale = 1.0 / float(width) ** 0.5
    projected = jnp.einsum(
        "tbij,bjk->tbik", left_ops, kept_block, preferred_element_type=jnp.float32
    ).astype(jnp.bfloat16)
    renormed = (
        jnp.einsum("bji,tbjk->tbik", kept_block, projected, preferred_element_type=jnp.float32)
        * out_scale
    ).astype(jnp.bfloat16)
    new_ops = shifted(renormed, "sec", 1)
    return (state, new_ops)


def solution(mesh):
    in_specs = (
        P("sec", None, None),
        P("op", "sec", None, None),
        P("op", "sec", None, None),
        P("sec"),
        P("op", "sec"),
        P("sec"),
    )
    out_specs = (P("sec", None, None), P("op", "sec", None, None))
    return jax.shard_map(
        per_device, mesh=mesh, in_specs=in_specs, out_specs=out_specs, check_vma=False
    )
```

profile of v0, /device:TPU:1, one launch (start us, length us, event | category | flops | bytes accessed | tf_op | source)
XLA Modules:
  0.0 1021.9 jit_solution(1389676207874550599)
XLA Ops:
  9.8 6.2 collective-permute-start.1
  16.9 5.3 collective-permute-done
  25.2 4.3 fusion.47
  30.5 62.1 %all-reduce.9.cloned.1.call-done = f32[2,256,256]{2,1,0:T(8,128)} async-done(((f32[2,256,256]{2,1,0:T(8,128)}), f32[2,256,256]{2,1,0:T(8,128)}) %all-reduce.9.cloned.1.call-update) | async-done | bytes 524304 | tf_op jit(solution)/shard_map/psum | solution.py:51
  95.3 78.5 %all-reduce.3 = (f32[]{:T(128)}, f32[]{:T(128)}) all-reduce(f32[]{:T(128)} %get-tuple-element.13, f32[]{:T(128)} %get-tuple-element.12), channel_id=1, replica_groups=mesh['sec'=32,'op'=8] {'sec','op'}, use_global_device_ids=true, to_apply=%region_2.0 | all-reduce | flops 2 | bytes 16 | tf_op jit(solution)/shard_map/psum | solution.py:53
  176.5 73.4 %psum.115 = f32[]{:T(128)} all-reduce(f32[]{:T(128)} %multiply_reduce_fusion.9), channel_id=1, replica_groups=mesh['sec'=32,'op'=8] {'sec','op'}, use_global_device_ids=true, to_apply=%region_6.0 | all-reduce | flops 1 | bytes 8 | tf_op jit(solution)/shard_map/psum | solution.py:63
  253.7 5.0 collective-permute-done.3
  258.8 5.2 collective-permute-done.2
  266.0 4.3 fusion.54
  270.4 57.5 %all-reduce.11.cloned.1.call-done = f32[2,256,256]{2,1,0:T(8,128)} async-done(((f32[2,256,256]{2,1,0:T(8,128)}), f32[2,256,256]{2,1,0:T(8,128)}) %all-reduce.11.cloned.1.call-update) | async-done | bytes 524304 | tf_op jit(solution)/shard_map/psum | solution.py:51
  330.6 78.5 %all-reduce.2 = (f32[]{:T(128)}, f32[]{:T(128)}) all-reduce(f32[]{:T(128)} %get-tuple-element.11, f32[]{:T(128)} %get-tuple-element.10), channel_id=1, replica_groups=mesh['sec'=32,'op'=8] {'sec','op'}, use_global_device_ids=true, to_apply=%region_9.0 | all-reduce | flops 2 | bytes 16 | tf_op jit(solution)/shard_map/psum | solution.py:53
  411.9 73.4 %psum.119 = f32[]{:T(128)} all-reduce(f32[]{:T(128)} %multiply_reduce_fusion.6), channel_id=1, replica_groups=mesh['sec'=32,'op'=8] {'sec','op'}, use_global_device_ids=true, to_apply=%region_13.0 | all-reduce | flops 1 | bytes 8 | tf_op jit(solution)/shard_map/psum | solution.py:63
  489.1 5.0 collective-permute-done.5
  494.1 5.2 collective-permute-done.4
  505.8 57.6 %all-reduce.13.cloned.1.call-done = f32[2,256,256]{2,1,0:T(8,128)} async-done(((f32[2,256,256]{2,1,0:T(8,128)}), f32[2,256,256]{2,1,0:T(8,128)}) %all-reduce.13.cloned.1.call-update) | async-done | bytes 524304 | tf_op jit(solution)/shard_map/psum | solution.py:51
  566.0 78.5 %all-reduce.1 = (f32[]{:T(128)}, f32[]{:T(128)}) all-reduce(f32[]{:T(128)} %get-tuple-element.9, f32[]{:T(128)} %get-tuple-element.8), channel_id=1, replica_groups=mesh['sec'=32,'op'=8] {'sec','op'}, use_global_device_ids=true, to_apply=%region_16.0 | all-reduce | flops 2 | bytes 16 | tf_op jit(solution)/shard_map/psum | solution.py:53
  647.3 73.4 %psum.123 = f32[]{:T(128)} all-reduce(f32[]{:T(128)} %multiply_reduce_fusion.3), channel_id=1, replica_groups=mesh['sec'=32,'op'=8] {'sec','op'}, use_global_device_ids=true, to_apply=%region_20.0 | all-reduce | flops 1 | bytes 8 | tf_op jit(solution)/shard_map/psum | solution.py:63
  724.5 5.0 collective-permute-done.7
  729.5 5.2 collective-permute-done.6
  741.1 57.6 %all-reduce.15.cloned.1.call-done = f32[2,256,256]{2,1,0:T(8,128)} async-done(((f32[2,256,256]{2,1,0:T(8,128)}), f32[2,256,256]{2,1,0:T(8,128)}) %all-reduce.15.cloned.1.call-update) | async-done | bytes 524304 | tf_op jit(solution)/shard_map/psum | solution.py:51
  801.4 78.5 %all-reduce = (f32[]{:T(128)}, f32[]{:T(128)}) all-reduce(f32[]{:T(128)} %get-tuple-element.7, f32[]{:T(128)} %get-tuple-element.6), channel_id=1, replica_groups=mesh['sec'=32,'op'=8] {'sec','op'}, use_global_device_ids=true, to_apply=%region_23.0 | all-reduce | flops 2 | bytes 16 | tf_op jit(solution)/shard_map/psum | solution.py:53
  882.7 73.4 %psum.127 = f32[]{:T(128)} all-reduce(f32[]{:T(128)} %multiply_reduce_fusion), channel_id=1, replica_groups=mesh['sec'=32,'op'=8] {'sec','op'}, use_global_device_ids=true, to_apply=%region_27.0 | all-reduce | flops 1 | bytes 8 | tf_op jit(solution)/shard_map/psum | solution.py:63
  957.0 4.3 fusion.40
  962.3 49.2 %collective-permute-done.8 = bf16[8,2,256,256]{2,3,0,1:T(8,128)(2,1)} collective-permute-done((bf16[8,2,256,256]{2,3,0,1:T(8,128)(2,1)}, bf16[8,2,256,256]{2,3,0,1:T(8,128)(2,1)}, u32[]{:S(2)}, u32[]{:S(2)}) %collective-permute-start.8) | collective-permute-done | bytes 2097184 | tf_op jit(solution)/shard_map/ppermute | solution.py:29
  (60 shorter events, 53.2 us)
Async XLA Ops:
  7.2 18.0 %copy-start = (bf16[8,2,256,256]{3,2,1,0:T(8,128)(2,1)S(1)}, bf16[8,2,256,256]{3,2,1,0:T(8,128)(2,1)}, u32[]{:S(2)}) copy-start(bf16[8,2,256,256]{3,2,1,0:T(8,128)(2,1)} %param.8) | copy-start | bytes 6291460
  7.2 85.4 %all-reduce.9.cloned.1.call-start = ((), (), s32[]{:S(2)}) async-start(), calls=%async_computation | async-start | bytes 1048576 | tf_op jit(solution)/shard_map/psum | solution.py:51
  7.2 14.9 %collective-permute-start = (bf16[2,256,256]{2,1,0:T(8,128)(2,1)}, bf16[2,256,256]{2,1,0:T(8,128)(2,1)S(1)}, u32[]{:S(2)}, u32[]{:S(2)}) collective-permute-start(bf16[2,256,256]{2,1,0:T(8,128)(2,1)} %param.6), channel_id=1, source_target_pairs={{0,8},{8,16},{16,24},{24,32},{32,40},{40,48},{48,56},{56,64},{64,7... | collective-permute-start | bytes 786440 | tf_op jit(solution)/shard_map/ppermute | solution.py:17
  9.8 12.4 %collective-permute-start.1 = (bf16[2,256,256]{2,1,0:T(8,128)(2,1)}, bf16[2,256,256]{2,1,0:T(8,128)(2,1)S(1)}, u32[]{:S(2)}, u32[]{:S(2)}) collective-permute-start(bf16[2,256,256]{2,1,0:T(8,128)(2,1)} %param.6), channel_id=1, source_target_pairs={{8,0},{16,8},{24,16},{32,24},{40,32},{48,40},{56,48},{64,56},{72,6... | collective-permute-start | bytes 786440 | tf_op jit(solution)/shard_map/ppermute | solution.py:19
  25.2 4.4 copy-start.1
  25.2 67.4 %copy-start.3 = (f32[2]{0:T(128)S(1)}, f32[2]{0:T(128)}, u32[]{:S(2)}) copy-start(f32[2]{0:T(128)} %param.9) | copy-start | bytes 28
  29.6 298.4 %all-reduce.11.cloned.1.call-start = ((), (), s32[]{:S(2)}) async-start(), calls=%async_computation.1 | async-start | bytes 1048576 | tf_op jit(solution)/shard_map/psum | solution.py:51
  251.6 7.2 collective-permute-start.3
  253.7 10.2 collective-permute-start.2
  270.3 293.0 %all-reduce.13.cloned.1.call-start = ((), (), s32[]{:S(2)}) async-start(), calls=%async_computation.2 | async-start | bytes 1048576 | tf_op jit(solution)/shard_map/psum | solution.py:51
  486.9 7.2 collective-permute-start.5
  489.1 10.2 collective-permute-start.4
  505.7 293.0 %all-reduce.15.cloned.1.call-start = ((), (), s32[]{:S(2)}) async-start(), calls=%async_computation.3 | async-start | bytes 1048576 | tf_op jit(solution)/shard_map/psum | solution.py:51
  722.3 7.2 collective-permute-start.7
  724.5 10.2 collective-permute-start.6
  741.1 141.5 %copy-start.4 = (s32[2]{0:T(128)S(1)}, s32[2]{0:T(128)}, u32[]{:S(2)}) copy-start(s32[2]{0:T(128)} %param.11) | copy-start | bytes 28
  957.0 4.3 copy-start.2
  961.3 50.2 %collective-permute-start.8 = (bf16[8,2,256,256]{2,3,0,1:T(8,128)(2,1)}, bf16[8,2,256,256]{2,3,0,1:T(8,128)(2,1)}, u32[]{:S(2)}, u32[]{:S(2)}) collective-permute-start(bf16[8,2,256,256]{2,3,0,1:T(8,128)(2,1)} %fusion.40), channel_id=1, source_target_pairs={{248,0},{0,8},{8,16},{16,24},{24,32},{32,40},{40,48},{48,56},{56,6... | collective-permute-start | bytes 6291464 | tf_op jit(solution)/shard_map/ppermute | solution.py:29
Sparse Core Ops, SparseCore 0:
  29.7 62.8 all-reduce.8
  270.5 57.4 all-reduce.10
  505.8 57.4 all-reduce.12
  741.2 57.4 all-reduce.14
where the time goes:
time: 1020 us
  blocking collectives  608 us (60%)
  waiting for transfers between devices  320 us (31%)
  other arithmetic  22.3 us (2%)
  between operations  22.1 us (2%)
  matrix products  21.6 us (2%)
  starting transfers between devices  16.4 us (2%)
  local copies, waits for them, and re-layouts  12.1 us (1%)
    psum x4, blocking collectives, per_device(): lax.psum((jnp.sum(state_part * sigma_part), jnp.sum(state_part * state_pa...  314 us
    psum x4, blocking collectives, per_device(): new_norm = lax.psum(jnp.sum(updated_part * updated_part), ('sec', 'op'))  294 us
    psum x4, waiting for transfers between devices, per_device(): sigma = lax.psum(partial_sigma, 'op') + shift_col * state_wide  235 us
    ppermute x1, waiting for transfers between devices, shifted(): return lax.ppermute(block, axis, route)  49.2 us
    ppermute x4, waiting for transfers between devices, padded(): lax.ppermute(tail, axis, [(i, (i + 1) % count) for i in range(count)])  20.8 us
  transfers between devices with their start and end apart: 13, of which 12 were waited for; matrix products, arithmetic and copies ran while one was open for 0% of the time, Pallas kernels for 0%

commit v1 on v0

--- a/solution.py
+++ b/solution.py
@@ -51,12 +51,15 @@
         sigma = lax.psum(partial_sigma, "op") + shift_col * state_wide
         sigma_part = lax.dynamic_slice_in_dim(sigma, share_start, share_rows, 1)
         energy_sum, norm_sum, square_sum = lax.psum(
-            (
-                jnp.sum(state_part * sigma_part),
-                jnp.sum(state_part * state_part),
-                jnp.sum(sigma_part * sigma_part),
+            lax.psum(
+                (
+                    jnp.sum(state_part * sigma_part),
+                    jnp.sum(state_part * state_part),
+                    jnp.sum(sigma_part * sigma_part),
+                ),
+                "sec",
             ),
-            ("sec", "op"),
+            "op",
         )
         ratio = energy_sum / norm_sum
         updated_part = state_part - step_size * (sigma_part - ratio * state_part)

time: 1020 us -> 1070 us (1.049)
  blocking collectives: 608 us -> 654 us
    psum x0 -> x4, blocking collectives: none -> 116 us  [per_device(): lax.psum(lax.psum((jnp.sum(state_part * sigma_part), jnp.sum(state_part *...]
    psum x4, blocking collectives: 314 us -> 247 us  [per_device(): lax.psum((jnp.sum(state_part * sigma_part), jnp.sum(state_part * state_pa...]
where the time goes in v1:
time: 1070 us
  blocking collectives  654 us (61%)
  waiting for transfers between devices  317 us (30%)
  other arithmetic  22.2 us (2%)
  between operations  22.1 us (2%)
  matrix products  21.6 us (2%)
  starting transfers between devices  18.2 us (2%)
  local copies, waits for them, and re-layouts  12.1 us (1%)
    psum x4, blocking collectives, per_device(): new_norm = lax.psum(jnp.sum(updated_part * updated_part), ('sec', 'op'))  290 us
    psum x4, blocking collectives, per_device(): lax.psum((jnp.sum(state_part * sigma_part), jnp.sum(state_part * state_pa...  247 us
    psum x4, waiting for transfers between devices, per_device(): sigma = lax.psum(partial_sigma, 'op') + shift_col * state_wide  233 us
    psum x4, blocking collectives, per_device(): lax.psum(lax.psum((jnp.sum(state_part * sigma_part), jnp.sum(state_part *...  116 us
    ppermute x1, waiting for transfers between devices, shifted(): return lax.ppermute(block, axis, route)  48.4 us
  transfers between devices with their start and end apart: 13, of which 12 were waited for; matrix products, arithmetic and copies ran while one was open for 0% of the time, Pallas kernels for 0%

profile of v1, /device:TPU:1, one launch (start us, length us, event | category | flops | bytes accessed | tf_op | source)
XLA Modules:
  0.0 1066.6 jit_solution(4058062092823648857)
XLA Ops:
  9.8 6.2 collective-permute-start.1
  16.9 5.3 collective-permute-done
  30.5 62.1 %all-reduce.13.cloned.1.call-done = f32[2,256,256]{2,1,0:T(8,128)} async-done(((f32[2,256,256]{2,1,0:T(8,128)}), f32[2,256,256]{2,1,0:T(8,128)}) %all-reduce.13.cloned.1.call-update) | async-done | bytes 524304 | tf_op jit(solution)/shard_map/psum | solution.py:51
  95.2 61.7 %all-reduce.3 = (f32[]{:T(128)}, f32[]{:T(128)}) all-reduce(f32[]{:T(128)} %get-tuple-element.13, f32[]{:T(128)} %get-tuple-element.12), channel_id=1, replica_groups=mesh['sec'=32,'op'=8] {'sec'}, use_global_device_ids=true, to_apply=%region_2.0 | all-reduce | flops 2 | bytes 16 | tf_op jit(solution)/shard_map/psum | solution.py:54
  156.9 29.1 %all-reduce.7 = (f32[]{:T(128)}, f32[]{:T(128)}) all-reduce(f32[]{:T(128)} %get-tuple-element.20, f32[]{:T(128)} %get-tuple-element.21), channel_id=1, replica_groups=mesh['sec'=32,'op'=8] {'op'}, use_global_device_ids=true, to_apply=%region_3.0 | all-reduce | flops 2 | bytes 16 | tf_op jit(solution)/shard_map/psum | solution.py:53
  188.8 72.6 %psum.173 = f32[]{:T(128)} all-reduce(f32[]{:T(128)} %multiply_reduce_fusion.9), channel_id=1, replica_groups=mesh['sec'=32,'op'=8] {'sec','op'}, use_global_device_ids=true, to_apply=%region_8.0 | all-reduce | flops 1 | bytes 8 | tf_op jit(solution)/shard_map/psum | solution.py:66
  265.5 5.3 collective-permute-done.3
  270.8 4.9 collective-permute-done.2
  282.2 56.8 %all-reduce.15.cloned.1.call-done = f32[2,256,256]{2,1,0:T(8,128)} async-done(((f32[2,256,256]{2,1,0:T(8,128)}), f32[2,256,256]{2,1,0:T(8,128)}) %all-reduce.15.cloned.1.call-update) | async-done | bytes 524304 | tf_op jit(solution)/shard_map/psum | solution.py:51
  341.6 61.6 %all-reduce.2 = (f32[]{:T(128)}, f32[]{:T(128)}) all-reduce(f32[]{:T(128)} %get-tuple-element.11, f32[]{:T(128)} %get-tuple-element.10), channel_id=1, replica_groups=mesh['sec'=32,'op'=8] {'sec'}, use_global_device_ids=true, to_apply=%region_11.0 | all-reduce | flops 2 | bytes 16 | tf_op jit(solution)/shard_map/psum | solution.py:54
  403.3 29.1 %all-reduce.6 = (f32[]{:T(128)}, f32[]{:T(128)}) all-reduce(f32[]{:T(128)} %get-tuple-element.18, f32[]{:T(128)} %get-tuple-element.19), channel_id=1, replica_groups=mesh['sec'=32,'op'=8] {'op'}, use_global_device_ids=true, to_apply=%region_12.0 | all-reduce | flops 2 | bytes 16 | tf_op jit(solution)/shard_map/psum | solution.py:53
  435.2 72.6 %psum.179 = f32[]{:T(128)} all-reduce(f32[]{:T(128)} %multiply_reduce_fusion.6), channel_id=1, replica_groups=mesh['sec'=32,'op'=8] {'sec','op'}, use_global_device_ids=true, to_apply=%region_17.0 | all-reduce | flops 1 | bytes 8 | tf_op jit(solution)/shard_map/psum | solution.py:66
  511.9 5.3 collective-permute-done.5
  517.2 4.9 collective-permute-done.4
  528.6 56.8 %all-reduce.17.cloned.1.call-done = f32[2,256,256]{2,1,0:T(8,128)} async-done(((f32[2,256,256]{2,1,0:T(8,128)}), f32[2,256,256]{2,1,0:T(8,128)}) %all-reduce.17.cloned.1.call-update) | async-done | bytes 524304 | tf_op jit(solution)/shard_map/psum | solution.py:51
  588.0 61.8 %all-reduce.1 = (f32[]{:T(128)}, f32[]{:T(128)}) all-reduce(f32[]{:T(128)} %get-tuple-element.9, f32[]{:T(128)} %get-tuple-element.8), channel_id=1, replica_groups=mesh['sec'=32,'op'=8] {'sec'}, use_global_device_ids=true, to_apply=%region_20.0 | all-reduce | flops 2 | bytes 16 | tf_op jit(solution)/shard_map/psum | solution.py:54
  649.8 29.1 %all-reduce.5 = (f32[]{:T(128)}, f32[]{:T(128)}) all-reduce(f32[]{:T(128)} %get-tuple-element.16, f32[]{:T(128)} %get-tuple-element.17), channel_id=1, replica_groups=mesh['sec'=32,'op'=8] {'op'}, use_global_device_ids=true, to_apply=%region_21.0 | all-reduce | flops 2 | bytes 16 | tf_op jit(solution)/shard_map/psum | solution.py:53
  681.8 72.6 %psum.185 = f32[]{:T(128)} all-reduce(f32[]{:T(128)} %multiply_reduce_fusion.3), channel_id=1, replica_groups=mesh['sec'=32,'op'=8] {'sec','op'}, use_global_device_ids=true, to_apply=%region_26.0 | all-reduce | flops 1 | bytes 8 | tf_op jit(solution)/shard_map/psum | solution.py:66
  758.5 5.3 collective-permute-done.7
  775.1 56.8 %all-reduce.19.cloned.1.call-done = f32[2,256,256]{2,1,0:T(8,128)} async-done(((f32[2,256,256]{2,1,0:T(8,128)}), f32[2,256,256]{2,1,0:T(8,128)}) %all-reduce.19.cloned.1.call-update) | async-done | bytes 524304 | tf_op jit(solution)/shard_map/psum | solution.py:51
  834.6 61.6 %all-reduce = (f32[]{:T(128)}, f32[]{:T(128)}) all-reduce(f32[]{:T(128)} %get-tuple-element.7, f32[]{:T(128)} %get-tuple-element.6), channel_id=1, replica_groups=mesh['sec'=32,'op'=8] {'sec'}, use_global_device_ids=true, to_apply=%region_29.0 | all-reduce | flops 2 | bytes 16 | tf_op jit(solution)/shard_map/psum | solution.py:54
  896.3 29.1 %all-reduce.4 = (f32[]{:T(128)}, f32[]{:T(128)}) all-reduce(f32[]{:T(128)} %get-tuple-element.14, f32[]{:T(128)} %get-tuple-element.15), channel_id=1, replica_groups=mesh['sec'=32,'op'=8] {'op'}, use_global_device_ids=true, to_apply=%region_30.0 | all-reduce | flops 2 | bytes 16 | tf_op jit(solution)/shard_map/psum | solution.py:53
  928.3 72.6 %psum.191 = f32[]{:T(128)} all-reduce(f32[]{:T(128)} %multiply_reduce_fusion), channel_id=1, replica_groups=mesh['sec'=32,'op'=8] {'sec','op'}, use_global_device_ids=true, to_apply=%region_35.0 | all-reduce | flops 1 | bytes 8 | tf_op jit(solution)/shard_map/psum | solution.py:66
  1007.8 48.4 %collective-permute-done.8 = bf16[8,2,256,256]{2,3,0,1:T(8,128)(2,1)} collective-permute-done((bf16[8,2,256,256]{2,3,0,1:T(8,128)(2,1)}, bf16[8,2,256,256]{2,3,0,1:T(8,128)(2,1)}, u32[]{:S(2)}, u32[]{:S(2)}) %collective-permute-start.8) | collective-permute-done | bytes 2097184 | tf_op jit(solution)/shard_map/ppermute | solution.py:29
  (64 shorter events, 72.8 us)
Async XLA Ops:
  7.2 18.0 %copy-start = (bf16[8,2,256,256]{3,2,1,0:T(8,128)(2,1)S(1)}, bf16[8,2,256,256]{3,2,1,0:T(8,128)(2,1)}, u32[]{:S(2)}) copy-start(bf16[8,2,256,256]{3,2,1,0:T(8,128)(2,1)} %param.8) | copy-start | bytes 6291460
  7.2 85.4 %all-reduce.13.cloned.1.call-start = ((), (), s32[]{:S(2)}) async-start(), calls=%async_computation | async-start | bytes 1048576 | tf_op jit(solution)/shard_map/psum | solution.py:51
  7.2 14.9 %collective-permute-start = (bf16[2,256,256]{2,1,0:T(8,128)(2,1)}, bf16[2,256,256]{2,1,0:T(8,128)(2,1)S(1)}, u32[]{:S(2)}, u32[]{:S(2)}) collective-permute-start(bf16[2,256,256]{2,1,0:T(8,128)(2,1)} %param.6), channel_id=1, source_target_pairs={{0,8},{8,16},{16,24},{24,32},{32,40},{40,48},{48,56},{56,64},{64,7... | collective-permute-start | bytes 786440 | tf_op jit(solution)/shard_map/ppermute | solution.py:17
  9.8 12.4 %collective-permute-start.1 = (bf16[2,256,256]{2,1,0:T(8,128)(2,1)}, bf16[2,256,256]{2,1,0:T(8,128)(2,1)S(1)}, u32[]{:S(2)}, u32[]{:S(2)}) collective-permute-start(bf16[2,256,256]{2,1,0:T(8,128)(2,1)} %param.6), channel_id=1, source_target_pairs={{8,0},{16,8},{24,16},{32,24},{40,32},{48,40},{56,48},{64,56},{72,6... | collective-permute-start | bytes 786440 | tf_op jit(solution)/shard_map/ppermute | solution.py:19
  25.2 4.4 copy-start.1
  25.2 67.4 %copy-start.3 = (f32[2]{0:T(128)S(1)}, f32[2]{0:T(128)}, u32[]{:S(2)}) copy-start(f32[2]{0:T(128)} %param.9) | copy-start | bytes 28
  29.6 309.4 %all-reduce.15.cloned.1.call-start = ((), (), s32[]{:S(2)}) async-start(), calls=%async_computation.1 | async-start | bytes 1048576 | tf_op jit(solution)/shard_map/psum | solution.py:51
  263.0 7.8 collective-permute-start.3
  265.5 10.2 collective-permute-start.2
  282.1 303.3 %all-reduce.17.cloned.1.call-start = ((), (), s32[]{:S(2)}) async-start(), calls=%async_computation.2 | async-start | bytes 1048576 | tf_op jit(solution)/shard_map/psum | solution.py:51
  509.4 7.8 collective-permute-start.5
  511.9 10.2 collective-permute-start.4
  528.5 303.4 %all-reduce.19.cloned.1.call-start = ((), (), s32[]{:S(2)}) async-start(), calls=%async_computation.3 | async-start | bytes 1048576 | tf_op jit(solution)/shard_map/psum | solution.py:51
  756.0 7.8 collective-permute-start.7
  758.5 10.2 collective-permute-start.6
  775.1 153.1 %copy-start.4 = (s32[2]{0:T(128)S(1)}, s32[2]{0:T(128)}, u32[]{:S(2)}) copy-start(s32[2]{0:T(128)} %param.11) | copy-start | bytes 28
  1001.7 4.3 copy-start.2
  1006.0 50.2 %collective-permute-start.8 = (bf16[8,2,256,256]{2,3,0,1:T(8,128)(2,1)}, bf16[8,2,256,256]{2,3,0,1:T(8,128)(2,1)}, u32[]{:S(2)}, u32[]{:S(2)}) collective-permute-start(bf16[8,2,256,256]{2,3,0,1:T(8,128)(2,1)} %fusion.40), channel_id=1, source_target_pairs={{248,0},{0,8},{8,16},{16,24},{24,32},{32,40},{40,48},{48,56},{56,6... | collective-permute-start | bytes 6291464 | tf_op jit(solution)/shard_map/ppermute | solution.py:29
Sparse Core Ops, SparseCore 0:
  29.7 62.8 all-reduce.12
  282.2 56.6 all-reduce.14
  528.7 56.6 all-reduce.16
  775.2 56.6 all-reduce.18
